TPU v7x, 128 devices: a whole 4x4x4 slice. The times are simulated.
128 devices in a mesh: pipe: 4 (over z_hi, core), tensor: 8 (over z_lo, y), dp: 4 (over x).
Axes of the slice: x: 4, y: 4, z: 4 (z_hi: 2, z_lo: 2; z = z_hi * 2 + z_lo), core: 2. Of those that a mesh axis runs over, the one named last changes fastest.
Arguments:
- tokens: bfloat16 [4, 1024, 4096], P('pipe', ('tensor', 'dp')), may hold values from -6 to 6
- grad_out: bfloat16 [4, 1024, 4096], P('pipe', ('tensor', 'dp')), may hold values from -6 to 6
- weights_in: bfloat16 [4, 2, 14336, 4096], P('pipe', None, ('tensor', 'dp')), may hold values from -0.09375 to 0.09375
- weights_down: bfloat16 [4, 14336, 4096], P('pipe', ('tensor', 'dp')), may hold values from -0.046875 to 0.046875
- projector: bfloat16 [4, 4096, 512], P('pipe'), may hold values from -0.25 to 0.25
- moment_first: float32 [4, 14336, 512], P('pipe', ('tensor', 'dp')), may hold values from -60 to 60
- moment_second: float32 [4, 14336, 512], P('pipe', ('tensor', 'dp')), may hold values from 1 to 10
Outputs:
- grad_prev: bfloat16 [4, 1024, 4096], P('pipe', ('tensor', 'dp'))
- update: bfloat16 [4, 14336, 4096], P('pipe', ('tensor', 'dp'))
All inputs are finite; a program needn't handle non-finite values.
Results may differ from a plain program's by a relative error of at most 0.0064.
Values may be sent and summed in bfloat16 or wider, within the bound.
A program may use at most 128 MiB of HBM per device.

v0:
```python
import jax
import jax.numpy as jnp
from jax import lax
from jax.sharding import PartitionSpec as P

beta_one = 0.9
beta_two = 0.999
bias_one = 1.0 - 0.9**10
bias_two = 1.0 - 0.999**10
epsilon = 1e-08


def in_one_piece(arrays, axis, dim, along):
    ends, at = ([], 0)
    for a in arrays[:-1]:
        at += a.shape[along]
        ends.append(at)
    both = jnp.concatenate(arrays, axis=along)
    return tuple(jnp.split(lax.all_gather(both, axis, axis=dim, tiled=True), ends, axis=along))


def shifted(value, axis, steps):
    count = lax.axis_size(axis)
    pairs = [(source, (source + steps) % count) for source in range(count)]
    return lax.ppermute(value, axis, pairs)


def adam_update(low_grad, moment_first, moment_second, projector):
    first_moment = beta_one * moment_first + (1.0 - beta_one) * low_grad
    second_moment = beta_two * moment_second + (1.0 - beta_two) * low_grad * low_grad
    normed = (first_moment / bias_one / (jnp.sqrt(second_moment / bias_two) + epsilon)).astype(
        jnp.bfloat16
    )
    return lax.dot_general(
        normed, projector, (((1,), (1,)), ((), ())), preferred_element_type=jnp.float32
    ).astype(jnp.bfloat16)


def local_backward(all_tokens, all_grads, all_proj, weights_in, weights_down):
    pre_act = jnp.einsum("kfd,nd->kfn", weights_in, all_tokens, preferred_element_type=jnp.float32)
    gate_pre = pre_act[0]
    up_act = pre_act[1]
    sigmoid_gate = jax.nn.sigmoid(gate_pre)
    silu_gate = gate_pre * sigmoid_gate
    hidden = (silu_gate * up_act).astype(jnp.bfloat16)
    grad_hidden = lax.dot_general(
        weights_down, all_grads, (((1,), (1,)), ((), ())), preferred_element_type=jnp.float32
    )
    grad_gate = (
        grad_hidden * up_act * sigmoid_gate * (1.0 + gate_pre * (1.0 - sigmoid_gate))
    ).astype(jnp.bfloat16)
    grad_up = (grad_hidden * silu_gate).astype(jnp.bfloat16)
    both_grads = jnp.stack([grad_gate, grad_up])
    partial_in = jnp.einsum(
        "kfn,kfd->nd", both_grads, weights_in, preferred_element_type=jnp.float32
    )
    low_grad = jnp.dot(hidden, all_proj, preferred_element_type=jnp.float32)
    return (partial_in, low_grad)


def per_device(tokens, grad_out, weights_in, weights_down, projector, moment_first, moment_second):
    own_tokens = tokens[0]
    own_grads = grad_out[0]
    local_in = weights_in[0]
    local_down = weights_down[0]
    local_proj = projector[0]
    own_proj = jnp.dot(own_grads, local_proj, preferred_element_type=jnp.float32).astype(
        jnp.bfloat16
    )
    all_tokens, all_grads, all_proj = in_one_piece(
        (own_tokens, own_grads, own_proj), ("tensor", "dp"), 0, 1
    )
    partial_in, low_grad = local_backward(all_tokens, all_grads, all_proj, local_in, local_down)
    grad_in = lax.psum_scatter(partial_in, ("tensor", "dp"), scatter_dimension=0, tiled=True)
    passed = shifted(grad_in.astype(jnp.bfloat16), "pipe", -1)
    update = adam_update(low_grad, moment_first[0], moment_second[0], local_proj)
    return (passed[None], update[None])


def solution(mesh):
    return jax.shard_map(
        per_device,
        mesh=mesh,
        in_specs=(
            P("pipe", ("tensor", "dp"), None),
            P("pipe", ("tensor", "dp"), None),
            P("pipe", None, ("tensor", "dp"), None),
            P("pipe", ("tensor", "dp"), None),
            P("pipe", None, None),
            P("pipe", ("tensor", "dp"), None),
            P("pipe", ("tensor", "dp"), None),
        ),
        out_specs=(P("pipe", ("tensor", "dp"), None), P("pipe", ("tensor", "dp"), None)),
        check_vma=False,
    )
```

profile of v0, /device:TPU:1, one launch (start us, length us, event | category | flops | bytes accessed | tf_op | source)
XLA Modules:
  0.0 467.3 jit_solution(2626270794295040567)
XLA Ops:
  7.2 0.0 copy-start
  7.2 0.0 copy-start.1
  7.2 0.0 all-gather.2.cloned.1.call-start
  7.2 3.1 fusion.21
  10.3 0.0 copy-done
  10.4 0.0 copy-done.1
  10.4 0.8 pad_maximum_fusion
  11.2 0.0 all-gather.2.cloned.1.call-update
  11.2 0.0 reduce-scatter.2.cloned.1.call-start
  11.3 204.6 %all-gather.2.cloned.1.call-done = bf16[1024,8704]{1,0:T(8,128)(2,1)} async-done(((bf16[32,8704]{1,0:T(8,128)(2,1)}), bf16[1024,8704]{1,0:T(8,128)(2,1)}) %all-gather.2.cloned.1.call-update) | async-done | bytes 17825808 | tf_op jit(solution)/shard_map/all_gather | solution.py:19
  215.9 0.0 copy-start.2
  215.9 0.0 copy-start.3
  215.9 11.5 %fusion.10 = f32[2,448,1024]{2,1,0:T(8,128)S(1)} fusion(bf16[1,2,448,4096]{3,2,1,0:T(8,128)(2,1)} %param.9, bf16[1024,8704]{1,0:T(8,128)(2,1)} %all-gather.2.cloned.1.call-done), kind=kOutput, calls=%fused_computation.13 | convolution fusion | flops 7516192768 | bytes 19398656 | tf_op jit(solution)/shard_map/kfd,nd->kfn/dot_general | solution.py:40
  227.4 0.0 copy-done.2
  227.4 0.1 copy-done.3
  227.5 0.0 copy-start.6
  227.5 4.4 fusion.34
  232.0 0.0 copy-done.6
  232.0 14.5 %convolution_bitcast_fusion = f32[1024,4096]{1,0:T(8,128)} fusion(bf16[1,2,448,4096]{3,2,1,0:T(8,128)(2,1)} %param.9, bf16[1,448,1024]{2,1,0:T(8,128)(2,1)S(1)} %get-tuple-element.3, bf16[1,448,1024]{2,1,0:T(8,128)(2,1)S(1)} %get-tuple-element.2), kind=kOutput, calls=%fused_computation | convolution fusion | flops 7517110272 | bytes 25952256 | tf_op jit(solution)/shard_map/kfn,kfd->nd/dot_general | solution.py:54
  246.5 0.0 copy-start.4
  246.5 0.0 copy-start.5
  246.5 0.0 reduce-scatter.2.cloned.1.call-update
  246.5 184.9 %reduce-scatter.2.cloned.1.call-done = f32[32,4096]{1,0:T(8,128)} async-done(((f32[1024,4096]{1,0:T(8,128)}), f32[32,4096]{1,0:T(8,128)}) %reduce-scatter.2.cloned.1.call-update) | async-done | bytes 524304 | tf_op jit(solution)/shard_map/reduce_scatter | solution.py:74
  431.4 1.1 convert_element_type.24
  432.4 18.7 %collective-permute-start = (bf16[32,4096]{1,0:T(8,128)(2,1)S(1)}, bf16[32,4096]{1,0:T(8,128)(2,1)S(1)}, u32[]{:S(2)}, u32[]{:S(2)}) collective-permute-start(bf16[32,4096]{1,0:T(8,128)(2,1)S(1)} %convert_element_type.24), channel_id=1, source_target_pairs={{0,96},{32,0},{64,32},{96,64},{1,97},{33,1},{65,33},{97,65},{2,98}... | collective-permute-start | bytes 786440 | tf_op jit(solution)/shard_map/ppermute | solution.py:25
  451.1 0.0 copy-done.4
  451.1 0.0 copy-done.5
  451.1 8.6 %fusion.5 = bf16[1,448,4096]{2,1,0:T(8,128)(2,1)} fusion(bf16[1,4096,512]{2,1,0:T(8,128)(2,1)} %param.11, f32[1,448,512]{2,1,0:T(8,128)S(1)} %copy-done.4, f32[1,448,512]{2,1,0:T(8,128)S(1)} %copy-done.5, bf16[1024,8704]{1,0:T(8,128)(2,1)} %all-gather.2.cloned.1.call-done, f32[2,448,1024]{2,1,0:T(8,128)} %copy-done.6), kind=kOutput, calls=%fused_computation.8 | convolution fusion | flops 2356150272 | bytes 14417920 | tf_op jit(solution)/shard_map/dot_general | solution.py:34
  459.8 0.0 collective-permute-done
  459.8 0.7 copy.10
Async XLA Ops:
  7.2 3.2 copy-start
  7.2 3.2 copy-start.1
  7.2 208.7 %all-gather.2.cloned.1.call-start = ((), (), s32[]{:S(2)}) async-start(), calls=%async_computation.1 | async-start | bytes 18382848 | tf_op jit(solution)/shard_map/all_gather | solution.py:19
  11.2 420.1 %reduce-scatter.2.cloned.1.call-start = ((), (), s32[]{:S(2)}) async-start(), calls=%async_computation.2 | async-start | bytes 17301504 | tf_op jit(solution)/shard_map/reduce_scatter | solution.py:74
  215.9 11.6 %copy-start.2 = (bf16[1024,8704]{1,0:T(8,128)(2,1)S(1)}, bf16[1024,8704]{1,0:T(8,128)(2,1)}, u32[]{:S(2)}) copy-start(bf16[1024,8704]{1,0:T(8,128)(2,1)} %all-gather.2.cloned.1.call-done) | copy-start | bytes 53477380
  215.9 11.7 %copy-start.3 = (bf16[1,448,4096]{2,1,0:T(8,128)(2,1)S(1)}, bf16[1,448,4096]{2,1,0:T(8,128)(2,1)}, u32[]{:S(2)}) copy-start(bf16[1,448,4096]{2,1,0:T(8,128)(2,1)} %param.10) | copy-start | bytes 11010052
  227.5 4.4 copy-start.6
  246.5 204.7 %copy-start.4 = (f32[1,448,512]{2,1,0:T(8,128)S(1)}, f32[1,448,512]{2,1,0:T(8,128)}, u32[]{:S(2)}) copy-start(f32[1,448,512]{2,1,0:T(8,128)} %param.13) | copy-start | bytes 2752516
  246.5 204.7 %copy-start.5 = (f32[1,448,512]{2,1,0:T(8,128)S(1)}, f32[1,448,512]{2,1,0:T(8,128)}, u32[]{:S(2)}) copy-start(f32[1,448,512]{2,1,0:T(8,128)} %param.12) | copy-start | bytes 2752516
  432.4 27.3 %collective-permute-start = (bf16[32,4096]{1,0:T(8,128)(2,1)S(1)}, bf16[32,4096]{1,0:T(8,128)(2,1)S(1)}, u32[]{:S(2)}, u32[]{:S(2)}) collective-permute-start(bf16[32,4096]{1,0:T(8,128)(2,1)S(1)} %convert_element_type.24), channel_id=1, source_target_pairs={{0,96},{32,0},{64,32},{96,64},{1,97},{33,1},{65,33},{97,65},{2,98}... | collective-permute-start | bytes 786440 | tf_op jit(solution)/shard_map/ppermute | solution.py:25
Sparse Core Ops, SparseCore 0:
  11.4 204.4 all-gather.1
  246.6 184.7 reduce-scatter.1
where the time goes:
time: 467 us
  waiting for transfers between devices  389 us (83%)
  matrix products  42.2 us (9%)
  starting transfers between devices  18.8 us (4%)
  between operations  14.1 us (3%)
    all_gather x1, waiting for transfers between devices, in_one_piece(): lax.all_gather(both, axis, axis=dim, tiled=True)  205 us
    reduce_scatter x1, waiting for transfers between devices, per_device(): lax.psum_scatter(partial_in, ('tensor', 'dp'), scatter_dimension=0, tiled...  185 us
    ppermute x1, starting transfers between devices, shifted(): return lax.ppermute(value, axis, pairs)  18.7 us
    dot_general x1, matrix products, local_backward(): jnp.einsum('kfn,kfd->nd', both_grads, weights_in, preferred_element_type=...  14.5 us
    dot_general x1, matrix products, local_backward(): jnp.einsum('kfd,nd->kfn', weights_in, all_tokens, preferred_element_type=...  11.5 us
  transfers between devices with their start and end apart: 3, of which 2 were waited for; matrix products, arithmetic and copies ran while one was open for 2% of the time, Pallas kernels for 0%

commit v1 on v0

v1 whole, which is shorter than its diff:
```python
import functools

import jax
import jax.numpy as jnp
from jax import lax
from jax.experimental import pallas as pl
from jax.experimental.pallas import tpu as pltpu
from jax.sharding import PartitionSpec as P

beta_one = 0.9
beta_two = 0.999
bias_one = 1.0 - 0.9**10
bias_two = 1.0 - 0.999**10
epsilon = 1e-08

MESH = pl.DeviceIdType.MESH
bf16, f32 = jnp.bfloat16, jnp.float32
D, FF, RANK = 4096, 448, 512
ROWS = 16
C1 = 2816
S1 = 2816
CT = 1024
UT = 1024
NT = (((1,), (1,)), ((), ()))
NN = (((1,), (0,)), ((), ()))


def dot(a, b, dims=NN):
    return lax.dot_general(a, b, dims, preferred_element_type=f32)


def kernel(tok, grd, win, wdn, prj, mom1, mom2, out_prev, out_upd,
           buf, WI, WD, PR, M1, M2, part, R1, R2o, R2, R3o, R3, R4,
           GA, UA, HI, GT, TA, PC, LG, NM, US,
           lsem, wsem, usem, recv, sent):
    pipe = lax.axis_index("pipe")
    t = lax.axis_index("tensor")
    x = lax.axis_index("dp")
    z0, y = t // 4, t % 4
    z1 = 1 - z0
    Z = (z0, z1)
    L0, M0 = (y, x), (x, y)

    def dev(h, l, m, z):
        return {"tensor": z * 4 + (l if h == 0 else m), "dp": m if h == 0 else l}

    def to(v, d):
        return (v + 1 + 2 * d) % 4

    def frm(v, d):
        return (v + 3 + 2 * d) % 4

    def ldev(h, d):
        return dev(h, to(L0[h], d), M0[h], z0)

    def mdev(h, d):
        return dev(h, L0[h], to(M0[h], d), z0)

    zdev = dev(0, L0[0], M0[0], z1)
    pdev = {"pipe": (pipe + 3) % 4}
    barrier = pltpu.get_barrier_semaphore()
    for h in (0, 1):
        for d in (0, 1):
            pl.semaphore_signal(barrier, inc=1, device_id=ldev(h, d), device_id_type=MESH)
    pl.semaphore_signal(barrier, inc=1, device_id=zdev, device_id_type=MESH)
    for step in (1, 3):
        pl.semaphore_signal(
            barrier, inc=1, device_id={"pipe": (pipe + step) % 4}, device_id_type=MESH
        )

    own = [
        pltpu.make_async_copy(
            src.at[0, h * ROWS : (h + 1) * ROWS, :],
            buf.at[h, L0[h], z0, M0[h], a],
            lsem.at[h, a],
        )
        for h in (0, 1)
        for a, src in ((0, tok), (1, grd))
    ]
    for c in own:
        c.start()
    loads = [
        pltpu.make_async_copy(src.at[0], dst, wsem.at[i])
        for i, (src, dst) in enumerate(((win, WI), (wdn, WD), (prj, PR), (mom1, M1), (mom2, M2)))
    ]
    for c in loads:
        c.start()
    LG[...] = jnp.zeros_like(LG)
    for c in own:
        c.wait()
    pl.semaphore_wait(barrier, 7)

    pending = []

    def send(src, dst, name, idx, to_dev):
        c = pltpu.make_async_remote_copy(
            src, dst, sent[name].at[idx], recv[name].at[idx], device_id=to_dev, device_id_type=MESH
        )
        c.start()
        pending.append(c)

    def arrive(ref, name, idx):
        pltpu.make_async_remote_copy(
            ref, ref, sent[name].at[idx], recv[name].at[idx], device_id=zdev, device_id_type=MESH
        ).wait_recv()

    def rot(v, r):
        return (v + r) % 4

    def cols(zz, edge):
        return (0, D) if zz == 0 else (0, edge)

    def half(zz, d, edge):
        n = cols(zz, edge)[1] // 2
        return (0, n) if d == 0 else (n, 2 * n)

    def piece(h, l, zz, m, c):
        return buf.at[h, l, Z[zz], m, :, :, c[0] : c[1]]

    def gsend(h, l, zz, m, c, name, idx, to_dev):
        r = piece(h, l, zz, m, c)
        send(r, r, name, idx, to_dev)

    def l_spread(h, zz, mr):
        for d in (0, 1):
            gsend(h, L0[h], zz, rot(M0[h], mr), cols(zz, C1), "gl", (h, zz, mr, d), ldev(h, d))

    def m_spread(h, zz):
        for d in (0, 1):
            gsend(h, L0[h], zz, M0[h], cols(zz, C1), "gm", (h, zz, d), mdev(h, d))

    def z_forward(h, lr, mr):
        gsend(h, rot(L0[h], lr), 0, rot(M0[h], mr), (C1, D), "gy", (h, lr, mr), zdev)

    def on_m(zz):
        for h in (0, 1):
            for d in (0, 1):
                o = frm(M0[h], d)
                arrive(piece(h, L0[h], zz, o, cols(zz, C1)), "gm", (h, zz, d))
                gsend(h, L0[h], zz, o, half(zz, d, C1), "gmo", (h, zz, d), mdev(h, d))
                l_spread(h, zz, 3 - 2 * d)
                if zz == 0:
                    z_forward(h, 0, 3 - 2 * d)

    def on_mo(zz):
        for h in (0, 1):
            for d in (0, 1):
                arrive(
                    piece(h, L0[h], zz, rot(M0[h], 2), half(zz, d, C1)), "gmo", (h, zz, d)
                )
            l_spread(h, zz, 2)
            if zz == 0:
                z_forward(h, 0, 2)

    def on_z():
        for h in (0, 1):
            arrive(piece(h, L0[h], 1, M0[h], (0, D)), "gz", (h,))
            m_spread(h, 1)
            l_spread(h, 1, 0)

    def on_l(zz, mr):
        for h in (0, 1):
            m = rot(M0[h], mr)
            for d in (0, 1):
                o = frm(L0[h], d)
                arrive(piece(h, o, zz, m, cols(zz, C1)), "gl", (h, zz, mr, d))
                gsend(h, o, zz, m, half(zz, d, C1), "glo", (h, zz, mr, d), ldev(h, d))
                if zz == 0:
                    z_forward(h, 3 - 2 * d, mr)

    def on_lo(zz, mr):
        for h in (0, 1):
            m = rot(M0[h], mr)
            for d in (0, 1):
                arrive(
                    piece(h, rot(L0[h], 2), zz, m, half(zz, d, C1)), "glo", (h, zz, mr, d)
                )
            if zz == 0:
                z_forward(h, 2, mr)

    def on_y(lr, mrs):
        for mr in mrs:
            for h in (0, 1):
                arrive(
                    piece(h, rot(L0[h], lr), 1, rot(M0[h], mr), (C1, D)), "gy", (h, lr, mr)
                )

    def rows_of(lr, a):
        return jnp.concatenate(
            [buf[h, rot(L0[h], lr), :, :, a].reshape(8 * ROWS, D) for h in (0, 1)], 0
        )

    def t_gate(lr):
        GA[...] = dot(WI[0], rows_of(lr, 0), NT)

    def t_up(lr):
        UA[...] = dot(WI[1], rows_of(lr, 0), NT)

    def t_act(lr):
        gh = dot(WD[...], rows_of(lr, 1), NT)
        g, u = GA[...], UA[...]
        s = 1.0 / (1.0 + jnp.exp(-g))
        silu = g * s
        HI[...] = (silu * u).astype(bf16)
        GT[0] = (gh * u * s * (1.0 + g * (1.0 - s))).astype(bf16)
        GT[1] = (gh * silu).astype(bf16)

    def t_turn(lr):
        TA[0] = GT[0].T
        TA[1] = GT[1].T

    def t_low(lr):
        PC[...] = dot(rows_of(lr, 1), PR[...]).astype(bf16)
        LG[...] += dot(HI[...], PC[...])

    def t_in(lr, j):
        c = slice(j * CT, (j + 1) * CT)
        r = (dot(TA[0], WI[0, :, c]) + dot(TA[1], WI[1, :, c])).astype(bf16)
        for h in (0, 1):
            part[h, rot(L0[h], lr), :, :, :, c] = r[h * 128 : (h + 1) * 128].reshape(
                2, 4, ROWS, CT
            )

    def pview(h, l, zz, m, c):
        return part.at[h, l, Z[zz], m, :, c[0] : c[1]]

    def add(h, l, zz, m, c, *refs):
        v = pview(h, l, zz, m, c)
        total = v[...].astype(f32)
        for r in refs:
            total += r[...].astype(f32)
        v[...] = total.astype(bf16)

    def y_send(lr):
        for h in (0, 1):
            for mr in range(4):
                l, m = rot(L0[h], lr), rot(M0[h], mr)
                send(pview(h, l, 1, m, (S1, D)), R1.at[h, lr, mr], "ry", (h, lr, mr), zdev)

    def y_add(lr, mr):
        for h in (0, 1):
            l, m = rot(L0[h], lr), rot(M0[h], mr)
            r = R1.at[h, lr, mr]
            arrive(r, "ry", (h, lr, mr))
            add(h, l, 0, m, (S1, D), r)

    def lo_send(zz, mr, d):
        for h in (0, 1):
            c = half(zz, d, S1)
            n = c[1] - c[0]
            v = pview(h, rot(L0[h], 2), zz, rot(M0[h], mr), c)
            send(v, R2o.at[h, zz, mr, d, :, 0:n], "rlo", (h, zz, mr, d), ldev(h, d))

    def lo_add(zz, mr):
        for h in (0, 1):
            for d in (0, 1):
                c = half(zz, d, S1)
                r = R2o.at[h, zz, mr, d, :, 0 : c[1] - c[0]]
                arrive(r, "rlo", (h, zz, mr, d))
                l, m = to(L0[h], d), rot(M0[h], mr)
                add(h, l, zz, m, c, r)
                f = cols(zz, S1)
                send(
                    pview(h, l, zz, m, f),
                    R2.at[h, zz, mr, d, :, 0 : f[1]],
                    "rl",
                    (h, zz, mr, d),
                    ldev(h, d),
                )

    def l_add(zz, mr):
        f = cols(zz, S1)
        for h in (0, 1):
            rs = [R2.at[h, zz, mr, d, :, 0 : f[1]] for d in (0, 1)]
            for d in (0, 1):
                arrive(rs[d], "rl", (h, zz, mr, d))
            add(h, L0[h], zz, rot(M0[h], mr), f, *rs)

    def mo_send(zz):
        for h in (0, 1):
            for d in (0, 1):
                c = half(zz, d, S1)
                v = pview(h, L0[h], zz, rot(M0[h], 2), c)
                send(v, R3o.at[h, zz, d, :, 0 : c[1] - c[0]], "rmo", (h, zz, d), mdev(h, d))

    def mo_add(zz, d):
        for h in (0, 1):
            c, f = half(zz, d, S1), cols(zz, S1)
            r = R3o.at[h, zz, d, :, 0 : c[1] - c[0]]
            arrive(r, "rmo", (h, zz, d))
            m = to(M0[h], d)
            add(h, L0[h], zz, m, c, r)
            send(
                pview(h, L0[h], zz, m, f),
                R3.at[h, zz, d, :, 0 : f[1]],
                "rm",
                (h, zz, d),
                mdev(h, d),
            )

    def m_add(zz):
        f = cols(zz, S1)
        for h in (0, 1):
            rs = [R3.at[h, zz, d, :, 0 : f[1]] for d in (0, 1)]
            for d in (0, 1):
                arrive(rs[d], "rm", (h, zz, d))
            add(h, L0[h], zz, M0[h], f, *rs)

    def z_send():
        for h in (0, 1):
            send(pview(h, L0[h], 1, M0[h], (0, S1)), R4.at[h], "rz", (h,), zdev)

    def z_add():
        for h in (0, 1):
            arrive(R4.at[h], "rz", (h,))
            add(h, L0[h], 0, M0[h], (0, S1), R4.at[h])
            send(
                pview(h, L0[h], 0, M0[h], (0, D)),
                out_prev.at[0, h * ROWS : (h + 1) * ROWS, :],
                "out",
                (h,),
                pdev,
            )

    def adam():
        low = LG[...]
        first = beta_one * M1[...] + (1.0 - beta_one) * low
        second = beta_two * M2[...] + (1.0 - beta_two) * low * low
        NM[...] = (first / bias_one / (jnp.sqrt(second / bias_two) + epsilon)).astype(bf16)

    def u_copy(j):
        return pltpu.make_async_copy(
            US.at[j % 2], out_upd.at[0, :, j * UT : (j + 1) * UT], usem.at[j % 2]
        )

    def update(j):
        if j >= 2:
            u_copy(j - 2).wait()
        US[j % 2] = dot(NM[...], PR[j * UT : (j + 1) * UT, :], NT).astype(bf16)
        u_copy(j).start()

    for h in (0, 1):
        gsend(h, L0[h], 0, M0[h], (0, D), "gz", (h,), zdev)
        m_spread(h, 0)
    for h in (0, 1):
        l_spread(h, 0, 0)
    on_m(0)
    on_z()
    on_l(0, 0)
    on_mo(0)
    on_m(1)
    on_l(0, 3)
    on_l(0, 1)
    on_mo(1)
    on_lo(0, 0)
    on_y(0, (3, 1, 2))
    for c in loads:
        c.wait()
    t_gate(0)
    on_l(0, 2)
    t_up(0)
    on_l(1, 0)
    t_act(0)
    t_turn(0)
    on_l(1, 3)
    t_low(0)
    on_l(1, 1)
    t_in(0, 0)
    t_in(0, 1)
    on_lo(0, 3)
    t_in(0, 2)
    t_in(0, 3)
    on_lo(0, 1)
    on_l(1, 2)
    on_lo(0, 2)
    on_y(3, range(4))
    for lr, more in ((3, (0, 3)), (1, (1, 2))):
        if lr == 1:
            on_y(1, range(4))
        t_gate(lr)
        t_up(lr)
        t_act(lr)
        on_lo(1, more[0])
        t_turn(lr)
        t_low(lr)
        t_in(lr, 0)
        t_in(lr, 1)
        on_lo(1, more[1])
        t_in(lr, 2)
        t_in(lr, 3)
    on_y(2, range(4))
    for lr in (3, 1, 0):
        y_send(lr)
    t_gate(2)
    t_up(2)
    t_act(2)
    t_turn(2)
    for j in range(4):
        t_in(2, j)
    y_send(2)
    for mr in (2, 3, 1, 0):
        lo_send(1, mr, 0)
        lo_send(1, mr, 1)
        lo_send(0, mr, 0)
    t_low(2)
    for mr in (2, 3, 1, 0):
        y_add(2, mr)
        lo_send(0, mr, 1)
    adam()
    for mr in (2, 3, 1, 0):
        y_add(3, mr)
        y_add(1, mr)
        lo_add(1, mr)
        lo_add(0, mr)
        y_add(0, mr)
        update((2, 3, 1, 0).index(mr))
    for mr in (2, 3, 1, 0):
        for zz in (1, 0):
            l_add(zz, mr)
            if mr == 2:
                mo_send(zz)
            elif mr != 0:
                mo_add(zz, 0 if mr == 1 else 1)
    m_add(1)
    z_send()
    m_add(0)
    z_add()
    for j in (2, 3):
        u_copy(j).wait()
    for h in (0, 1):
        arrive(out_prev.at[0, h * ROWS : (h + 1) * ROWS, :], "out", (h,))
    for c in pending:
        c.wait_send()


SEMAPHORES = {
    "gz": (2,),
    "gm": (2, 2, 2),
    "gmo": (2, 2, 2),
    "gl": (2, 2, 4, 2),
    "glo": (2, 2, 4, 2),
    "gy": (2, 4, 4),
    "ry": (2, 4, 4),
    "rlo": (2, 2, 4, 2),
    "rl": (2, 2, 4, 2),
    "rmo": (2, 2, 2),
    "rm": (2, 2, 2),
    "rz": (2,),
    "out": (2,),
}


def per_device(*args):
    dma = pltpu.SemaphoreType.DMA
    vmem = pltpu.VMEM
    return pl.pallas_call(
        kernel,
        out_shape=(
            jax.ShapeDtypeStruct((1, 2 * ROWS, D), bf16),
            jax.ShapeDtypeStruct((1, FF, D), bf16),
        ),
        in_specs=[pl.BlockSpec(memory_space=pl.ANY)] * 7,
        out_specs=[pl.BlockSpec(memory_space=pl.ANY)] * 2,
        scratch_shapes=[
            vmem((2, 4, 2, 4, 2, ROWS, D), bf16),
            vmem((2, FF, D), bf16),
            vmem((FF, D), bf16),
            vmem((D, RANK), bf16),
            vmem((FF, RANK), f32),
            vmem((FF, RANK), f32),
            vmem((2, 4, 2, 4, ROWS, D), bf16),
            vmem((2, 4, 4, ROWS, D - S1), bf16),
            vmem((2, 2, 4, 2, ROWS, D // 2), bf16),
            vmem((2, 2, 4, 2, ROWS, D), bf16),
            vmem((2, 2, 2, ROWS, D // 2), bf16),
            vmem((2, 2, 2, ROWS, D), bf16),
            vmem((2, ROWS, S1), bf16),
            vmem((FF, 256), f32),
            vmem((FF, 256), f32),
            vmem((FF, 256), bf16),
            vmem((2, FF, 256), bf16),
            vmem((2, 256, FF), bf16),
            vmem((256, RANK), bf16),
            vmem((FF, RANK), f32),
            vmem((FF, RANK), bf16),
            vmem((2, FF, UT), bf16),
            dma((2, 2)),
            dma((5,)),
            dma((2,)),
            {k: dma(v) for k, v in SEMAPHORES.items()},
            {k: dma(v) for k, v in SEMAPHORES.items()},
        ],
        compiler_params=pltpu.CompilerParams(
            collective_id=0, has_side_effects=True, vmem_limit_bytes=63 * 2**20
        ),
    )(*args)


def solution(mesh):
    rows = P("pipe", ("tensor", "dp"), None)
    return jax.shard_map(
        per_device,
        mesh=mesh,
        in_specs=(rows, rows, P("pipe", None, ("tensor", "dp"), None), rows, P("pipe", None, None), rows, rows),
        out_specs=(rows, rows),
        check_vma=False,
    )
```

time: 467 us -> 177 us (0.38)
  waiting for transfers between devices: 389 us -> 0 us
  Pallas kernels: 0 us -> 170 us
  matrix products: 42.2 us -> 0 us
  starting transfers between devices: 18.8 us -> 0 us
  between operations: 14.1 us -> 0.64 us
  local copies, waits for them, and re-layouts: 0.85 us -> 5.96 us
    all_gather x1 -> x0, waiting for transfers between devices: 205 us -> none  [in_one_piece(): lax.all_gather(both, axis, axis=dim, tiled=True)]
    reduce_scatter x1 -> x0, waiting for transfers between devices: 185 us -> none  [per_device(): lax.psum_scatter(partial_in, ('tensor', 'dp'), scatter_dimension=0, tiled...]
    pallas_call x0 -> x1, Pallas kernels: none -> 170 us  [per_device(): pl.pallas_call(kernel, out_shape=(jax.ShapeDtypeStruct((1, 2 * ROWS, D),...]
    dot_general x5 -> x0, matrix products: 42.2 us -> none  [the longest x1 14.5 us: local_backward(): jnp.einsum('kfn,kfd->nd', both_grads, weights_in, preferred_element_type=...]
    ppermute x1 -> x0, starting transfers between devices: 18.7 us -> none  [shifted(): return lax.ppermute(value, axis, pairs)]
    unnamed x15 -> x2, local copies, waits for them, and re-layouts: 0.85 us -> 5.96 us
  transfers between devices with their start and end apart: 3 -> 0, of which waited for: 2 -> 0; matrix products, arithmetic and copies ran while one was open for 2% -> 0% of each run, Pallas kernels for 0% -> 0%
where the time goes in v1:
time: 177 us
  Pallas kernels  170 us (96%)
  local copies, waits for them, and re-layouts  5.96 us (3%)
    pallas_call x1, Pallas kernels, per_device(): pl.pallas_call(kernel, out_shape=(jax.ShapeDtypeStruct((1, 2 * ROWS, D),...  170 us
    unnamed x2, local copies, waits for them, and re-layouts  5.96 us

profile of v1, /device:TPU:1, one launch (start us, length us, event | category | flops | bytes accessed | tf_op | source)
XLA Modules:
  0.0 177.0 jit_solution(8584118948841827378)
XLA Ops:
  0.6 170.4 %shard_map.86 = (bf16[1,32,4096]{2,1,0:T(8,128)(2,1)}, bf16[1,448,4096]{2,1,0:T(8,128)(2,1)}) custom-call(bf16[1,32,4096]{2,1,0:T(8,128)(2,1)} %tok.1, bf16[1,32,4096]{2,1,0:T(8,128)(2,1)} %grd.1, bf16[1,2,448,4096]{3,2,1,0:T(8,128)(2,1)} %win.1, bf16[1,448,4096]{2,1,0:T(8,128)(2,1)} %wdn.1, bf16[1,4096,512]{2,1,0:T(8,128)(2,1)} %prj.1, ...), custom_call_target="tpu_custom_call" | custom-call | tf_op jit(solution)/shard_map/pallas_call | solution.py:456
  171.0 1.7 copy.11
  172.7 4.3 %copy.12 = bf16[1,448,4096]{2,1,0:T(8,128)(2,1)} copy(bf16[1,448,4096]{2,1,0:T(8,128)(2,1)} %get-tuple-element.5) | data formatting | bytes 7340032

commit v2 on v0

v2 whole, which is shorter than its diff:
```python
import functools

import jax
import jax.numpy as jnp
from jax import lax
from jax.experimental import pallas as pl
from jax.experimental.pallas import tpu as pltpu
from jax.sharding import PartitionSpec as P

beta_one = 0.9
beta_two = 0.999
bias_one = 1.0 - 0.9**10
bias_two = 1.0 - 0.999**10
epsilon = 1e-08

MESH = pl.DeviceIdType.MESH
bf16, f32 = jnp.bfloat16, jnp.float32
D, FF, RANK = 4096, 448, 512
ROWS = 16
C1 = 2816
S1 = 3072
CT = 1024
UT = 1024
NT = (((1,), (1,)), ((), ()))
NN = (((1,), (0,)), ((), ()))
CHUNKS = (0, 2, 1, 3)

KINDS = ("gz", "gm", "gmo", "gl", "glo", "gy", "ry", "rlo", "rl", "rmo", "rm", "rz", "out")
ORDER = (
    (2, 1, 0, 0), (2, 1, 0, 1), (2, 0, 0, 1), (2, 0, 0, 0), (1, 0), (4, 0, 0, 0, 0), (4, 0, 0, 0, 1),
    (4, 1, 0, 0, 1), (4, 1, 0, 0, 0), (1, 1), (0, 1, 1, 0, 0), (3, 1, 0, 0), (0, 1, 1, 0, 1), (3, 1, 0, 1),
    (0, 1, 0, 0, 1), (3, 0, 0, 1), (0, 0, 0), (2, 0, 1, 0), (6, 0, 0, 1), (0, 1, 0, 0, 0), (6, 0, 0, 3),
    (4, 0, 1, 0, 0), (4, 0, 1, 0, 1), (2, 0, 1, 1), (6, 1, 0, 1), (3, 0, 0, 0), (6, 1, 0, 3), (0, 0, 1),
    (2, 1, 1, 0), (2, 1, 1, 1), (4, 1, 1, 0, 1), (4, 1, 1, 0, 0), (0, 3, 0, 0, 0, 0), (6, 0, 3, 0),
    (0, 3, 1, 0, 0, 0), (6, 1, 3, 0), (5, 0, 0, 0, 0), (0, 3, 0, 0, 0, 1), (5, 0, 0, 0, 1),
    (0, 3, 1, 0, 0, 1), (5, 1, 0, 0, 1), (0, 1, 0, 1, 0), (3, 0, 1, 0), (6, 0, 1, 0), (6, 1, 1, 0),
    (5, 1, 0, 0, 0), (0, 3, 0, 1, 0, 0), (5, 0, 1, 0, 0), (0, 3, 0, 1, 0, 1), (5, 0, 1, 0, 1),
    (0, 1, 0, 1, 1), (3, 0, 1, 1), (0, 2, 0, 0), (6, 0, 0, 2), (4, 0, 0, 2, 0), (4, 0, 0, 2, 1),
    (0, 2, 1, 0), (4, 1, 0, 2, 1), (4, 1, 0, 2, 0), (6, 1, 0, 2), (0, 4, 0, 0, 0), (6, 0, 2, 0),
    (0, 1, 1, 1, 0), (3, 1, 1, 0), (0, 1, 1, 1, 1), (3, 1, 1, 1), (0, 4, 1, 0, 0), (6, 1, 2, 0),
    (0, 3, 1, 1, 0, 0), (5, 1, 1, 0, 0), (0, 3, 1, 1, 0, 1), (5, 1, 1, 0, 1), (0, 2, 0, 1), (4, 0, 1, 2, 0),
    (4, 0, 1, 2, 1), (4, 1, 0, 1, 1), (4, 1, 0, 1, 0), (0, 3, 0, 0, 2, 0), (6, 0, 3, 2), (0, 3, 0, 0, 2, 1),
    (6, 0, 1, 2), (5, 0, 0, 2, 0), (5, 0, 0, 2, 1), (0, 3, 1, 0, 2, 1), (6, 1, 1, 2), (0, 5, 0, 0),
    (0, 4, 0, 1, 0), (0, 5, 1, 0), (0, 4, 1, 1, 0), (7, 0), (4, 0, 0, 1, 0), (0, 2, 1, 1), (4, 1, 1, 2, 1),
    (4, 1, 1, 2, 0), (4, 0, 0, 1, 1), (8, 0), (0, 3, 1, 0, 2, 0), (6, 1, 3, 2), (9, 0), (10, 0),
    (5, 1, 0, 2, 1), (5, 1, 0, 2, 0), (12, 0, 0), (12, 0, 1), (12, 0, 2), (0, 3, 1, 0, 1, 0), (6, 1, 3, 1),
    (0, 3, 1, 0, 1, 1), (6, 1, 1, 1), (12, 0, 3), (0, 3, 0, 1, 2, 0), (5, 0, 1, 2, 0), (0, 3, 0, 1, 2, 1),
    (5, 0, 1, 2, 1), (4, 1, 1, 1, 0), (5, 1, 0, 1, 1), (11, 0), (0, 4, 0, 0, 2), (6, 0, 2, 2),
    (4, 0, 1, 1, 0), (4, 0, 1, 1, 1), (0, 3, 1, 1, 2, 1), (5, 1, 1, 2, 1), (13, 0, 1, 0), (13, 0, 2, 0),
    (0, 3, 1, 1, 2, 0), (5, 1, 1, 2, 0), (13, 0, 0, 0), (4, 1, 1, 1, 1), (13, 0, 3, 0), (0, 4, 1, 0, 2),
    (6, 1, 2, 2), (0, 3, 0, 0, 1, 0), (5, 0, 0, 1, 0), (0, 3, 0, 0, 1, 1), (5, 0, 0, 1, 1), (5, 1, 0, 1, 0),
    (6, 0, 3, 1), (4, 0, 0, 3, 0), (4, 0, 0, 3, 1), (4, 1, 0, 3, 1), (4, 1, 0, 3, 0), (6, 0, 1, 1),
    (13, 1, 0, 0), (0, 6, 0, 0), (14, 0, 2, 0), (14, 0, 0, 0), (14, 0, 1, 0), (14, 0, 3, 0), (13, 1, 1, 0),
    (13, 1, 3, 0), (0, 5, 0, 2), (0, 4, 0, 1, 2), (0, 5, 1, 2), (0, 4, 1, 1, 2), (7, 2), (13, 1, 2, 0),
    (8, 2), (0, 4, 0, 0, 1), (6, 0, 2, 1), (0, 3, 0, 1, 1, 0), (5, 0, 1, 1, 0), (0, 3, 0, 1, 1, 1),
    (5, 0, 1, 1, 1), (0, 3, 1, 1, 1, 0), (5, 1, 1, 1, 0), (0, 3, 1, 1, 1, 1), (5, 1, 1, 1, 1), (9, 2),
    (0, 4, 1, 0, 1), (6, 1, 2, 1), (4, 1, 1, 3, 0), (4, 0, 1, 3, 0), (4, 1, 1, 3, 1), (4, 0, 1, 3, 1),
    (10, 2), (12, 2, 0), (12, 2, 1), (12, 2, 2), (12, 2, 3), (0, 3, 0, 0, 3, 0), (5, 0, 0, 3, 0),
    (6, 0, 3, 3), (13, 0, 3, 2), (0, 3, 0, 0, 3, 1), (5, 0, 0, 3, 1), (0, 3, 1, 0, 3, 0), (5, 1, 0, 3, 0),
    (0, 3, 1, 0, 3, 1), (5, 1, 0, 3, 1), (0, 6, 1, 0), (14, 1, 1, 0), (14, 1, 2, 0), (14, 1, 0, 0),
    (14, 1, 3, 0), (13, 0, 0, 2), (11, 2), (13, 0, 1, 2), (13, 0, 2, 2), (6, 1, 3, 3), (15, 0, 1, 2, 0),
    (15, 0, 1, 0, 1), (15, 1, 1, 0, 1), (15, 1, 1, 0, 0), (0, 5, 0, 1), (0, 4, 0, 1, 1), (0, 5, 1, 1),
    (0, 4, 1, 1, 1), (7, 1), (15, 0, 1, 0, 0), (15, 1, 0, 0, 0), (15, 0, 0, 0, 1), (15, 1, 1, 2, 1), (8, 1),
    (6, 0, 1, 3), (15, 0, 0, 0, 0), (15, 1, 0, 0, 1), (9, 1), (0, 3, 0, 1, 3, 0), (5, 0, 1, 3, 0),
    (0, 3, 1, 1, 3, 0), (5, 1, 1, 3, 0), (0, 3, 0, 1, 3, 1), (5, 0, 1, 3, 1), (0, 3, 1, 1, 3, 1),
    (5, 1, 1, 3, 1), (6, 1, 1, 3), (10, 1), (12, 1, 0), (15, 1, 1, 2, 0), (15, 0, 1, 2, 1), (12, 1, 1),
    (0, 4, 1, 0, 3), (6, 1, 2, 3), (15, 0, 1, 1, 0), (15, 1, 1, 1, 0), (0, 6, 0, 2), (14, 0, 1, 2),
    (14, 0, 3, 2), (14, 0, 2, 2), (15, 0, 0, 2, 1), (14, 0, 0, 2), (12, 1, 2), (0, 4, 0, 0, 3), (6, 0, 2, 3),
    (15, 1, 0, 1, 0), (15, 0, 0, 1, 0), (15, 0, 1, 1, 1), (15, 1, 1, 1, 1), (0, 7, 1, 1, 0, 0),
    (16, 1, 1, 0, 0), (0, 7, 0, 1, 0, 1), (16, 0, 1, 0, 1), (0, 7, 1, 1, 0, 1), (16, 1, 1, 0, 1),
    (17, 1, 1, 0, 1), (0, 7, 0, 1, 0, 0), (16, 0, 1, 0, 0), (0, 7, 0, 1, 2, 0), (16, 0, 1, 2, 0),
    (17, 0, 1, 0, 1), (17, 0, 1, 2, 0), (17, 1, 1, 0, 0), (0, 7, 0, 0, 0, 1), (16, 0, 0, 0, 1),
    (0, 7, 1, 0, 0, 0), (16, 1, 0, 0, 0), (0, 7, 1, 1, 2, 1), (16, 1, 1, 2, 1), (12, 1, 3), (13, 0, 0, 1),
    (17, 1, 1, 2, 1), (0, 7, 0, 0, 0, 0), (16, 0, 0, 0, 0), (13, 0, 3, 1), (11, 1), (17, 0, 0, 0, 1),
    (13, 0, 1, 1), (13, 0, 2, 1), (17, 0, 1, 0, 0), (15, 1, 0, 2, 0), (0, 7, 1, 0, 0, 1), (16, 1, 0, 0, 1),
    (17, 1, 0, 0, 1), (0, 7, 0, 1, 2, 1), (16, 0, 1, 2, 1), (17, 1, 0, 0, 0), (0, 7, 1, 1, 2, 0),
    (16, 1, 1, 2, 0), (13, 1, 0, 2), (0, 7, 0, 1, 1, 0), (16, 0, 1, 1, 0), (17, 0, 1, 1, 0),
    (0, 7, 1, 1, 1, 0), (16, 1, 1, 1, 0), (13, 1, 3, 2), (0, 7, 1, 1, 1, 1), (16, 1, 1, 1, 1),
    (0, 7, 0, 0, 2, 1), (16, 0, 0, 2, 1), (17, 0, 1, 2, 1), (13, 1, 2, 2), (0, 7, 0, 1, 1, 1),
    (16, 0, 1, 1, 1), (17, 1, 1, 1, 1), (13, 1, 1, 2), (15, 0, 0, 2, 0), (17, 1, 1, 2, 0), (0, 5, 0, 3),
    (0, 4, 0, 1, 3), (0, 5, 1, 3), (0, 4, 1, 1, 3), (7, 3), (17, 0, 1, 1, 1), (13, 1, 1, 1), (13, 1, 3, 1),
    (8, 3), (17, 0, 0, 0, 0), (17, 1, 1, 1, 0), (13, 1, 2, 1), (13, 1, 0, 1), (0, 8, 1, 1, 0), (18, 1, 1, 0),
    (9, 3), (17, 0, 0, 2, 1), (0, 6, 0, 1), (14, 0, 1, 1), (0, 7, 0, 0, 1, 0), (16, 0, 0, 1, 0),
    (17, 0, 0, 1, 0), (14, 0, 2, 1), (14, 0, 0, 1), (14, 0, 3, 1), (0, 8, 0, 1, 0), (18, 0, 1, 0), (10, 3),
    (12, 3, 0), (15, 0, 0, 1, 1), (0, 8, 1, 0, 0), (18, 1, 0, 0), (0, 6, 1, 2), (14, 1, 3, 2), (14, 1, 0, 2),
    (14, 1, 1, 2), (0, 7, 1, 0, 2, 0), (16, 1, 0, 2, 0), (17, 1, 0, 2, 0), (14, 1, 2, 2), (15, 1, 0, 2, 1),
    (0, 7, 0, 0, 2, 0), (16, 0, 0, 2, 0), (17, 0, 0, 2, 0), (0, 8, 0, 1, 2), (18, 0, 1, 2), (19, 0, 1, 1),
    (12, 3, 1), (19, 0, 1, 0), (0, 8, 1, 1, 2), (18, 1, 1, 2), (19, 1, 1, 1), (0, 8, 0, 1, 1), (18, 0, 1, 1),
    (15, 1, 1, 3, 0), (0, 6, 1, 1), (14, 1, 1, 1), (0, 7, 1, 0, 1, 0), (16, 1, 0, 1, 0), (14, 1, 3, 1),
    (14, 1, 2, 1), (15, 1, 0, 1, 1), (14, 1, 0, 1), (12, 3, 2), (15, 0, 1, 3, 0), (15, 0, 1, 3, 1),
    (15, 1, 0, 3, 0), (15, 1, 1, 3, 1), (0, 8, 0, 0, 0), (18, 0, 0, 0), (19, 1, 1, 0), (0, 8, 1, 1, 1),
    (18, 1, 1, 1), (12, 3, 3), (13, 0, 0, 3), (13, 0, 1, 3), (13, 0, 3, 3), (15, 0, 0, 3, 0),
    (17, 1, 0, 1, 0), (11, 3), (13, 0, 2, 3), (13, 1, 1, 3), (13, 1, 0, 3), (0, 7, 0, 0, 1, 1),
    (16, 0, 0, 1, 1), (17, 0, 0, 1, 1), (0, 7, 1, 0, 2, 1), (16, 1, 0, 2, 1), (17, 1, 0, 2, 1), (27,),
    (13, 1, 3, 3), (13, 1, 2, 3), (0, 7, 1, 0, 1, 1), (16, 1, 0, 1, 1), (17, 1, 0, 1, 1), (0, 7, 1, 1, 3, 0),
    (16, 1, 1, 3, 0), (17, 1, 1, 3, 0), (0, 7, 0, 1, 3, 1), (16, 0, 1, 3, 1), (17, 0, 1, 3, 1),
    (0, 7, 0, 1, 3, 0), (16, 0, 1, 3, 0), (17, 0, 1, 3, 0), (0, 7, 1, 1, 3, 1), (16, 1, 1, 3, 1),
    (0, 9, 0, 1, 0), (20, 0, 1, 0), (21, 0, 1, 0), (0, 8, 0, 0, 2), (18, 0, 0, 2), (0, 9, 1, 1, 0),
    (20, 1, 1, 0), (21, 1, 1, 0), (28, 0), (17, 1, 1, 3, 1), (0, 6, 0, 3), (14, 0, 2, 3), (19, 0, 0, 0),
    (15, 0, 0, 3, 1), (14, 0, 3, 3), (14, 0, 0, 3), (14, 0, 1, 3), (0, 7, 0, 0, 3, 0), (16, 0, 0, 3, 0),
    (17, 0, 0, 3, 0), (28, 1), (19, 0, 0, 1), (0, 8, 0, 0, 1), (18, 0, 0, 1), (0, 8, 1, 0, 2), (18, 1, 0, 2),
    (19, 1, 0, 1), (28, 2), (19, 1, 0, 0), (0, 6, 1, 3), (14, 1, 1, 3), (0, 7, 1, 0, 3, 0), (16, 1, 0, 3, 0),
    (17, 1, 0, 3, 0), (14, 1, 2, 3), (15, 1, 0, 3, 1), (28, 3), (0, 8, 0, 1, 3), (18, 0, 1, 3),
    (0, 7, 0, 0, 3, 1), (16, 0, 0, 3, 1), (17, 0, 0, 3, 1), (14, 1, 3, 3), (14, 1, 0, 3), (0, 9, 0, 1, 1),
    (20, 0, 1, 1), (21, 0, 1, 1), (0, 8, 1, 0, 1), (18, 1, 0, 1), (0, 8, 1, 1, 3), (18, 1, 1, 3),
    (0, 9, 1, 1, 1), (20, 1, 1, 1), (21, 1, 1, 1), (0, 9, 0, 0, 0), (20, 0, 0, 0), (21, 0, 0, 0),
    (0, 7, 1, 0, 3, 1), (16, 1, 0, 3, 1), (17, 1, 0, 3, 1), (0, 9, 1, 0, 0), (20, 1, 0, 0), (21, 1, 0, 0),
    (0, 10, 0, 1), (22, 0, 1), (23, 0), (0, 8, 0, 0, 3), (18, 0, 0, 3), (0, 9, 0, 0, 1), (20, 0, 0, 1),
    (21, 0, 0, 1), (0, 10, 1, 1), (22, 1, 1), (23, 1), (0, 8, 1, 0, 3), (18, 1, 0, 3), (0, 9, 1, 0, 1),
    (20, 1, 0, 1), (21, 1, 0, 1), (0, 10, 0, 0), (22, 0, 0), (0, 11, 0), (24, 0), (25, 0), (0, 10, 1, 0),
    (22, 1, 0), (0, 11, 1), (24, 1), (25, 1), (0, 12, 0), (0, 12, 1),
)


def dot(a, b, dims=NN):
    return lax.dot_general(a, b, dims, preferred_element_type=f32)


def kernel(tok, grd, win, wdn, prj, mom1, mom2, out_prev, out_upd,
           buf, WI, WD, PR, M1, M2, part, R1, R2o, R2, R3o, R3, R4,
           GA, UA, HI, GT, TA, PC, LG, NM, US,
           lsem, wsem, usem, recv, sent):
    pipe = lax.axis_index("pipe")
    t = lax.axis_index("tensor")
    x = lax.axis_index("dp")
    z0, y = t // 4, t % 4
    z1 = 1 - z0
    Z = (z0, z1)
    L0, M0 = (y, x), (x, y)

    def dev(h, l, m, z):
        return {"tensor": z * 4 + (l if h == 0 else m), "dp": m if h == 0 else l}

    def to(v, d):
        return (v + 1 + 2 * d) % 4

    def ldev(h, d):
        return dev(h, to(L0[h], d), M0[h], z0)

    def mdev(h, d):
        return dev(h, L0[h], to(M0[h], d), z0)

    zdev = dev(0, L0[0], M0[0], z1)
    pdev = {"pipe": (pipe + 3) % 4}
    barrier = pltpu.get_barrier_semaphore()
    for h in (0, 1):
        for d in (0, 1):
            pl.semaphore_signal(barrier, inc=1, device_id=ldev(h, d), device_id_type=MESH)
    pl.semaphore_signal(barrier, inc=1, device_id=zdev, device_id_type=MESH)
    for step in (1, 3):
        pl.semaphore_signal(
            barrier, inc=1, device_id={"pipe": (pipe + step) % 4}, device_id_type=MESH
        )

    own = [
        pltpu.make_async_copy(
            src.at[0, h * ROWS : (h + 1) * ROWS, :],
            buf.at[h, M0[h], L0[h], z0, a],
            lsem.at[h, a],
        )
        for h in (0, 1)
        for a, src in ((0, tok), (1, grd))
    ]
    for c in own:
        c.start()
    loads = [
        pltpu.make_async_copy(src.at[0], dst, wsem.at[i])
        for i, (src, dst) in enumerate(((win, WI), (wdn, WD), (prj, PR), (mom1, M1), (mom2, M2)))
    ]
    for c in loads:
        c.start()
    for c in own:
        c.wait()
    pl.semaphore_wait(barrier, 7)

    def group(key):
        name = key[0]
        if name in ("gmo", "glo", "rl", "rm"):
            return name, key[1:-1]
        if name in ("gy", "ry"):
            return name, (key[1], key[3])
        return name, key[1:]

    def send(src, dst, key, to_dev):
        name, idx = group(key)
        c = pltpu.make_async_remote_copy(
            src,
            dst,
            sent.at[FAMILIES.index(family(key))],
            recv[name].at[idx],
            device_id=to_dev,
            device_id_type=MESH,
        )
        c.start()

    def rot(v, r):
        return (v + r) % 4

    def cols(zz, edge):
        return (0, D) if zz == 0 else (0, edge)

    def half(zz, d, edge):
        n = cols(zz, edge)[1] // 2
        return (0, n) if d == 0 else (n, 2 * n)

    def piece(h, lr, zz, mr, c):
        return buf.at[h, rot(M0[h], mr), rot(L0[h], lr), Z[zz], :, :, c[0] : c[1]]

    def psum(h, lr, zz, mr, c):
        return part.at[h, rot(M0[h], mr), rot(L0[h], lr), Z[zz], :, c[0] : c[1]]

    def landing(key):
        name, h, *rest = key
        if name == "gz":
            return piece(h, 0, 1, 0, (0, D))
        if name == "gm":
            zz, d = rest
            return piece(h, 0, zz, 3 - 2 * d, cols(zz, C1))
        if name == "gmo":
            zz, d = rest
            return piece(h, 0, zz, 2, half(zz, d, C1))
        if name == "gl":
            zz, mr, d = rest
            return piece(h, 3 - 2 * d, zz, mr, cols(zz, C1))
        if name == "glo":
            zz, mr, d = rest
            return piece(h, 2, zz, mr, half(zz, d, C1))
        if name == "gy":
            lr, mr = rest
            return piece(h, lr, 1, mr, (C1, D))
        if name == "ry":
            return R1.at[h, rest[1], rest[0]]
        if name == "rlo":
            zz, mr, d = rest
            return R2o.at[h, zz, mr, d, :, 0 : cols(zz, S1)[1] // 2]
        if name == "rl":
            zz, mr, d = rest
            return R2.at[h, zz, mr, d, :, 0 : cols(zz, S1)[1]]
        if name == "rmo":
            zz, d = rest
            return R3o.at[h, zz, d, :, 0 : cols(zz, S1)[1] // 2]
        if name == "rm":
            zz, d = rest
            return R3.at[h, zz, d, :, 0 : cols(zz, S1)[1]]
        if name == "rz":
            return R4.at[h]
        return out_prev.at[0, h * ROWS : (h + 1) * ROWS, :]

    def arrived(name, h, *rest):
        if name == "gmo":
            return piece(h, 0, rest[0], 2, cols(rest[0], C1))
        if name == "glo":
            return piece(h, 2, rest[0], rest[1], cols(rest[0], C1))
        if name == "gy":
            n = 3 if rest[0] == 0 else 4
            return buf.at[h, rot(M0[h], rest[0]), 0:n, z1, :, :, C1:D]
        if name == "ry":
            return R1.at[h, rest[0]]
        if name == "rl":
            return R2.at[h, rest[0], rest[1], :, :, 0 : cols(rest[0], S1)[1]]
        if name == "rm":
            return R3.at[h, rest[0], :, :, 0 : cols(rest[0], S1)[1]]
        return landing((name, h, *rest))

    def w(kind, *idx):
        name = KINDS[kind]
        ref = arrived(name, *idx)
        pltpu.make_async_remote_copy(
            ref, ref, sent.at[0], recv[name].at[idx], device_id=zdev, device_id_type=MESH
        ).wait_recv()

    def gsend(key, ref, to_dev):
        send(ref, ref, key, to_dev)

    def gz(h):
        gsend(("gz", h), piece(h, 0, 0, 0, (0, D)), zdev)

    def gm(h, zz, d):
        gsend(("gm", h, zz, d), piece(h, 0, zz, 0, cols(zz, C1)), mdev(h, d))

    def gmo(h, zz, d):
        gsend(("gmo", h, zz, d), piece(h, 0, zz, 3 - 2 * d, half(zz, d, C1)), mdev(h, d))

    def gl(h, zz, mr, d):
        gsend(("gl", h, zz, mr, d), piece(h, 0, zz, mr, cols(zz, C1)), ldev(h, d))

    def glo(h, zz, mr, d):
        gsend(("glo", h, zz, mr, d), piece(h, 3 - 2 * d, zz, mr, half(zz, d, C1)), ldev(h, d))

    def gy(h, lr, mr):
        gsend(("gy", h, lr, mr), piece(h, lr, 0, mr, (C1, D)), zdev)

    def rows_of(mr, a):
        return jnp.concatenate(
            [buf[h, rot(M0[h], mr), :, :, a].reshape(8 * ROWS, D) for h in (0, 1)], 0
        )

    def t_gate(mr):
        if mr == CHUNKS[0]:
            for c in loads[:3]:
                c.wait()
        GA[...] = dot(WI[0], rows_of(mr, 0), NT)

    def t_up(mr):
        UA[...] = dot(WI[1], rows_of(mr, 0), NT)

    def t_act(mr):
        gh = dot(WD[...], rows_of(mr, 1), NT)
        g, u = GA[...], UA[...]
        s = 1.0 / (1.0 + jnp.exp(-g))
        silu = g * s
        HI[...] = (silu * u).astype(bf16)
        GT[0] = (gh * u * s * (1.0 + g * (1.0 - s))).astype(bf16)
        GT[1] = (gh * silu).astype(bf16)

    def t_turn(mr):
        TA[0] = GT[0].T
        TA[1] = GT[1].T

    def t_low(mr):
        PC[...] = dot(rows_of(mr, 1), PR[...]).astype(bf16)
        low = dot(HI[...], PC[...])
        LG[...] = low if mr == CHUNKS[0] else LG[...] + low

    def t_in(mr, j):
        c = slice(j * CT, (j + 1) * CT)
        r = (dot(TA[0], WI[0, :, c]) + dot(TA[1], WI[1, :, c])).astype(bf16)
        for h in (0, 1):
            part[h, rot(M0[h], mr), :, :, :, c] = r[h * 128 : (h + 1) * 128].reshape(
                4, 2, ROWS, CT
            )

    def add(dst, *refs):
        total = dst[...].astype(f32)
        for r in refs:
            total += r[...].astype(f32)
        dst[...] = total.astype(bf16)

    def rsend(key, src, to_dev):
        send(src, landing(key), key, to_dev)

    def ry(h, lr, mr):
        rsend(("ry", h, lr, mr), psum(h, lr, 1, mr, (S1, D)), zdev)

    def y_add(h, lr, mr):
        add(psum(h, lr, 0, mr, (S1, D)), landing(("ry", h, lr, mr)))

    def rlo(h, zz, mr, d):
        rsend(("rlo", h, zz, mr, d), psum(h, 2, zz, mr, half(zz, d, S1)), ldev(h, d))

    def lo_add(h, zz, mr, d):
        add(psum(h, 1 + 2 * d, zz, mr, half(zz, d, S1)), landing(("rlo", h, zz, mr, d)))

    def rl(h, zz, mr, d):
        rsend(("rl", h, zz, mr, d), psum(h, 1 + 2 * d, zz, mr, cols(zz, S1)), ldev(h, d))

    def l_add(h, zz, mr):
        add(
            psum(h, 0, zz, mr, cols(zz, S1)),
            landing(("rl", h, zz, mr, 0)),
            landing(("rl", h, zz, mr, 1)),
        )

    def rmo(h, zz, d):
        rsend(("rmo", h, zz, d), psum(h, 0, zz, 2, half(zz, d, S1)), mdev(h, d))

    def mo_add(h, zz, d):
        add(psum(h, 0, zz, 1 + 2 * d, half(zz, d, S1)), landing(("rmo", h, zz, d)))

    def rm(h, zz, d):
        rsend(("rm", h, zz, d), psum(h, 0, zz, 1 + 2 * d, cols(zz, S1)), mdev(h, d))

    def m_add(h, zz):
        add(
            psum(h, 0, zz, 0, cols(zz, S1)),
            landing(("rm", h, zz, 0)),
            landing(("rm", h, zz, 1)),
        )

    def rz(h):
        rsend(("rz", h), psum(h, 0, 1, 0, (0, S1)), zdev)

    def z_add(h):
        add(psum(h, 0, 0, 0, (0, S1)), landing(("rz", h)))

    def out(h):
        rsend(("out", h), psum(h, 0, 0, 0, (0, D)), pdev)

    def adam():
        for c in loads[3:]:
            c.wait()
        low = LG[...]
        first = beta_one * M1[...] + (1.0 - beta_one) * low
        second = beta_two * M2[...] + (1.0 - beta_two) * low * low
        NM[...] = (first / bias_one / (jnp.sqrt(second / bias_two) + epsilon)).astype(bf16)

    def u_copy(j):
        return pltpu.make_async_copy(
            US.at[j % 2], out_upd.at[0, :, j * UT : (j + 1) * UT], usem.at[j % 2]
        )

    def update(j):
        if j >= 2:
            u_copy(j - 2).wait()
        US[j % 2] = dot(NM[...], PR[j * UT : (j + 1) * UT, :], NT).astype(bf16)
        u_copy(j).start()

    steps = (
        w, gz, gm, gmo, gl, glo, gy, t_gate, t_up, t_act, t_turn, t_low, t_in, ry, y_add, rlo, lo_add, rl, l_add,
        rmo, mo_add, rm, m_add, rz, z_add, out, None, adam, update,
    )
    for op, *rest in ORDER:
        steps[op](*rest)
    for j in (2, 3):
        u_copy(j).wait()

    for i, (name, sub) in enumerate(FAMILIES):
        if name in ("gz", "gm", "gmo", "gl", "glo", "gy"):
            n = D - C1 if name == "gy" else cols(sub, C1)[1] // (2 if name[-1] == "o" else 1)
            at = {"gz": (0, 0, 0), "gl": (0, slice(0, 2)), "glo": (0, slice(0, 2))}.get(
                name, (0, 0, slice(0, 4), 0)
            )
            if name == "gy":
                at = (slice(0, 2), slice(0, 4), slice(0, 3), 0) if sub else (slice(0, 2), slice(0, 3), 0, 0)
            ref = buf.at[at + (slice(None),) * (6 - len(at)) + (slice(0, n),)]
        else:
            n = {"ry": D - S1, "rz": S1, "out": D}.get(name) or cols(sub, S1)[1] // (
                2 if name[-1] == "o" else 1
            )
            at = {"ry": (slice(0, 2), slice(0, 4), slice(0, 4), 0), "rl": (0, slice(0, 2)), "rlo": (0, slice(0, 2))}.get(
                name, (0, 0, slice(0, 4), 0) if name[:2] == "rm" else (0, 0, 0)
            )
            ref = part.at[at + (slice(None),) * (5 - len(at)) + (slice(0, n),)]
        pltpu.make_async_remote_copy(
            ref, ref, sent.at[i], recv["gz"].at[0], device_id=zdev, device_id_type=MESH
        ).wait_send()


FAMILIES = [
    ("gz", 0), ("gm", 0), ("gm", 1), ("gmo", 0), ("gmo", 1), ("gl", 0), ("gl", 1), ("glo", 0), ("glo", 1),
    ("gy", 0), ("gy", 1), ("ry", 0), ("rlo", 0), ("rlo", 1), ("rl", 0), ("rl", 1), ("rmo", 0), ("rmo", 1),
    ("rm", 0), ("rm", 1), ("rz", 0), ("out", 0),
]


def family(key):
    name = key[0]
    if name in ("gz", "ry", "rz", "out"):
        return name, 0
    return name, min(key[2], 1)


SEMAPHORES = {"gz": (2,), "gm": (2, 2, 2), "gmo": (2, 2), "gl": (2, 2, 4, 2), "glo": (2, 2, 4), "gy": (2, 4), "ry": (2, 4), "rlo": (2, 2, 4, 2), "rl": (2, 2, 4), "rmo": (2, 2, 2), "rm": (2, 2), "rz": (2,), "out": (2,)}


SETTLE = 7


def settle(prev, upd, out_prev, out_upd, vp, vu, rsem, wsem):
    n = FF // SETTLE
    trips = [(upd, vu, out_upd, slice(i * n, (i + 1) * n)) for i in range(SETTLE)]
    trips.append((prev, vp, out_prev, slice(0, 2 * ROWS)))
    reads = [
        pltpu.make_async_copy(a.at[0, r], v.at[0, r], rsem.at[i])
        for i, (a, v, _, r) in enumerate(trips)
    ]
    writes = [
        pltpu.make_async_copy(v.at[0, r], o.at[0, r], wsem.at[i])
        for i, (_, v, o, r) in enumerate(trips)
    ]
    for c in reads:
        c.start()
    for a, b in zip(reads, writes):
        a.wait()
        b.start()
    for c in writes:
        c.wait()


def per_device(*args):
    dma = pltpu.SemaphoreType.DMA
    vmem = pltpu.VMEM
    prev, upd = pl.pallas_call(
        kernel,
        out_shape=(
            jax.ShapeDtypeStruct((1, 2 * ROWS, D), bf16),
            jax.ShapeDtypeStruct((1, FF, D), bf16),
        ),
        in_specs=[pl.BlockSpec(memory_space=pl.ANY)] * 7,
        out_specs=[pl.BlockSpec(memory_space=pl.ANY)] * 2,
        scratch_shapes=[
            vmem((2, 4, 4, 2, 2, ROWS, D), bf16),
            vmem((2, FF, D), bf16),
            vmem((FF, D), bf16),
            vmem((D, RANK), bf16),
            vmem((FF, RANK), f32),
            vmem((FF, RANK), f32),
            vmem((2, 4, 4, 2, ROWS, D), bf16),
            vmem((2, 4, 4, ROWS, D - S1), bf16),
            vmem((2, 2, 4, 2, ROWS, D // 2), bf16),
            vmem((2, 2, 4, 2, ROWS, D), bf16),
            vmem((2, 2, 2, ROWS, D // 2), bf16),
            vmem((2, 2, 2, ROWS, D), bf16),
            vmem((2, ROWS, S1), bf16),
            vmem((FF, 256), f32),
            vmem((FF, 256), f32),
            vmem((FF, 256), bf16),
            vmem((2, FF, 256), bf16),
            vmem((2, 256, FF), bf16),
            vmem((256, RANK), bf16),
            vmem((FF, RANK), f32),
            vmem((FF, RANK), bf16),
            vmem((2, FF, UT), bf16),
            dma((2, 2)),
            dma((5,)),
            dma((2,)),
            {k: dma(v) for k, v in SEMAPHORES.items()},
            dma((len(FAMILIES),)),
        ],
        compiler_params=pltpu.CompilerParams(
            collective_id=0, has_side_effects=True, vmem_limit_bytes=63 * 2**20
        ),
    )(*args)
    return pl.pallas_call(
        settle,
        out_shape=(
            jax.ShapeDtypeStruct(prev.shape, bf16),
            jax.ShapeDtypeStruct(upd.shape, bf16),
        ),
        in_specs=[pl.BlockSpec(memory_space=pl.ANY)] * 2,
        out_specs=[pl.BlockSpec(memory_space=pl.ANY)] * 2,
        scratch_shapes=[
            vmem(prev.shape, bf16),
            vmem(upd.shape, bf16),
            dma((SETTLE + 1,)),
            dma((SETTLE + 1,)),
        ],
        compiler_params=pltpu.CompilerParams(vmem_limit_bytes=63 * 2**20),
    )(prev, upd)


def solution(mesh):
    rows = P("pipe", ("tensor", "dp"), None)
    return jax.shard_map(
        per_device,
        mesh=mesh,
        in_specs=(rows, rows, P("pipe", None, ("tensor", "dp"), None), rows, P("pipe", None, None), rows, rows),
        out_specs=(rows, rows),
        check_vma=False,
    )
```

time: 467 us -> 136 us (0.29)
  waiting for transfers between devices: 389 us -> 0 us
  Pallas kernels: 0 us -> 135 us
  matrix products: 42.2 us -> 0 us
  starting transfers between devices: 18.8 us -> 0 us
  between operations: 14.1 us -> 0.82 us
    all_gather x1 -> x0, waiting for transfers between devices: 205 us -> none  [in_one_piece(): lax.all_gather(both, axis, axis=dim, tiled=True)]
    reduce_scatter x1 -> x0, waiting for transfers between devices: 185 us -> none  [per_device(): lax.psum_scatter(partial_in, ('tensor', 'dp'), scatter_dimension=0, tiled...]
    pallas_call x0 -> x2, Pallas kernels: none -> 135 us  [the longest x1 131 us: per_device(): pl.pallas_call(kernel, out_shape=(jax.ShapeDtypeStruct((1, 2 * ROWS, D),...]
    dot_general x5 -> x0, matrix products: 42.2 us -> none  [the longest x1 14.5 us: local_backward(): jnp.einsum('kfn,kfd->nd', both_grads, weights_in, preferred_element_type=...]
    ppermute x1 -> x0, starting transfers between devices: 18.7 us -> none  [shifted(): return lax.ppermute(value, axis, pairs)]
  transfers between devices with their start and end apart: 3 -> 0, of which waited for: 2 -> 0; matrix products, arithmetic and copies ran while one was open for 2% -> 0% of each run, Pallas kernels for 0% -> 0%
where the time goes in v2:
time: 136 us; the launch traced here: 135 us
  Pallas kernels  135 us (99%)
    pallas_call x1, Pallas kernels, per_device(): pl.pallas_call(kernel, out_shape=(jax.ShapeDtypeStruct((1, 2 * ROWS, D),...  131 us
    pallas_call x1, Pallas kernels, per_device(): pl.pallas_call(settle, out_shape=(jax.ShapeDtypeStruct(prev.shape, bf16),...  3.2 us

profile of v2, /device:TPU:1, one launch (start us, length us, event | category | flops | bytes accessed | tf_op | source)
XLA Modules:
  0.0 135.5 jit_solution(17632865388072936886)
XLA Ops:
  0.6 131.5 %shard_map.86 = (bf16[1,32,4096]{2,1,0:T(8,128)(2,1)}, bf16[1,448,4096]{2,1,0:T(8,128)(2,1)}) custom-call(bf16[1,32,4096]{2,1,0:T(8,128)(2,1)} %tok.1, bf16[1,32,4096]{2,1,0:T(8,128)(2,1)} %grd.1, bf16[1,2,448,4096]{3,2,1,0:T(8,128)(2,1)} %win.1, bf16[1,448,4096]{2,1,0:T(8,128)(2,1)} %wdn.1, bf16[1,4096,512]{2,1,0:T(8,128)(2,1)} %prj.1, ...), custom_call_target="tpu_custom_call" | custom-call | tf_op jit(solution)/shard_map/pallas_call | solution.py:483
  132.1 3.2 %shard_map.87 = (bf16[1,32,4096]{2,1,0:T(8,128)(2,1)}, bf16[1,448,4096]{2,1,0:T(8,128)(2,1)}) custom-call(bf16[1,32,4096]{2,1,0:T(8,128)(2,1)} %get-tuple-element.4.prev, bf16[1,448,4096]{2,1,0:T(8,128)(2,1)} %get-tuple-element.5.upd), custom_call_target="tpu_custom_call" | custom-call | tf_op jit(solution)/shard_map/pallas_call | solution.py:524
